TPU v7x, 256 devices: a whole 4x4x8 slice. The times are simulated.
256 devices in a mesh: dp: 8 (over x, y_hi), seq: 32 (over y_lo, z, core).
Axes of the slice: x: 4, y: 4 (y_hi: 2, y_lo: 2; y = y_hi * 2 + y_lo), z: 8, core: 2. Of those that a mesh axis runs over, the one named last changes fastest.
Arguments:
- inputs: bfloat16 [8, 16384, 1024], P('dp', 'seq'), may hold values from -6 to 6
- out_grad: bfloat16 [8, 16384, 1024], P('dp', 'seq'), may hold values from -6 to 6
- w_in: bfloat16 [1024, 3072], replicated, may hold values from -0.1875 to 0.1875
- taps: float32 [3, 3072], replicated, may hold values from -3 to 3
- filt: bfloat16 [64, 256, 1024], P(None, 'seq'), may hold values from -4 to 4
Outputs:
- mixed: bfloat16 [8, 16384, 1024], P('dp', 'seq')
- in_grad: bfloat16 [8, 16384, 1024], P('dp', 'seq')
- w_in_grad: float32 [1024, 3072], P('dp', 'seq')
- taps_grad: float32 [3, 3072], replicated
All inputs are finite; a program needn't handle non-finite values.
Results may differ from a plain program's by a relative error of at most 0.012.
Values may be sent and summed in bfloat16 or wider, within the bound.
A program may use at most 128 MiB of HBM per device.

v0:
```python
import math
import jax
import jax.numpy as jnp
from jax import lax
from jax.sharding import PartitionSpec as P

BLK = 256


def padded(cells, sides, width):
    for axis, dim in sides:
        count = lax.axis_size(axis)
        ends = count - 1
        head = lax.slice_in_dim(cells, 0, width, axis=dim)
        tail = lax.slice_in_dim(cells, cells.shape[dim] - width, cells.shape[dim], axis=dim)
        cells = jnp.concatenate(
            [
                lax.ppermute(tail, axis, [(i, (i + 1) % count) for i in range(ends)]),
                cells,
                lax.ppermute(head, axis, [((i + 1) % count, i) for i in range(ends)]),
            ],
            axis=dim,
        )
    return cells


def dct_table(count):
    rows = jnp.arange(count, dtype=jnp.float32)[:, None]
    cols = jnp.arange(count, dtype=jnp.float32)[None, :]
    first = jnp.where(rows == 0, jnp.float32(math.sqrt(0.5)), jnp.float32(1.0))
    table = (
        jnp.float32(math.sqrt(2.0 / count))
        * first
        * jnp.cos(jnp.float32(math.pi) * (cols + 0.5) * rows / count)
    )
    return table.astype(jnp.bfloat16)


def block_section(blocks, table_q):
    return jnp.einsum("rq,nbqd->nbrd", table_q, blocks, preferred_element_type=jnp.float32).astype(
        jnp.bfloat16
    )


def span_section(columns, filt, table_p):
    stack, span, narrow, width = columns.shape
    flat = columns.reshape(stack, span, narrow * width)
    second = jnp.einsum("ap,npk->nak", table_p, flat, preferred_element_type=jnp.float32)
    scaled = (filt.reshape(1, span, narrow * width).astype(jnp.float32) * second).astype(
        jnp.bfloat16
    )
    third = jnp.einsum("ap,nak->npk", table_p, scaled, preferred_element_type=jnp.float32).astype(
        jnp.bfloat16
    )
    return third.reshape(columns.shape)


def final_section(blocks, table_q):
    return jnp.einsum("rq,nbrd->nbqd", table_q, blocks, preferred_element_type=jnp.float32)


def shards(inputs, out_grad, w_in, taps, filt):
    tok = inputs.shape[1]
    width = inputs.shape[2]
    nseq = lax.axis_size("seq")
    ndata = lax.axis_size("dp")
    nblocks = tok // BLK
    table_q = dct_table(BLK)
    table_p = dct_table(filt.shape[0])
    factor = 1.0 / math.sqrt(ndata * nseq * tok)
    rows = inputs[0]
    z = jnp.dot(rows, w_in, preferred_element_type=jnp.float32).astype(jnp.bfloat16)
    zpad = padded(z, (("seq", 0),), 1)
    s = taps[0] * zpad[:-2] + taps[1] * zpad[1:-1] + taps[2] * zpad[2:]
    a_part = s[:, :width]
    g_part = s[:, width : 2 * width]
    v_part = s[:, 2 * width :]
    w = (a_part * v_part).astype(jnp.bfloat16)
    gradf = out_grad[0].astype(jnp.float32)
    e4 = (gradf * g_part).astype(jnp.bfloat16)
    columns = lax.all_to_all(
        block_section(w.reshape(1, nblocks, BLK, width), table_q),
        "seq",
        split_axis=2,
        concat_axis=1,
        tiled=True,
    )
    back = lax.all_to_all(
        span_section(columns, filt, table_p), "seq", split_axis=1, concat_axis=2, tiled=True
    )
    h4 = final_section(back, table_q).reshape(tok, width)
    grad_cols = lax.all_to_all(
        block_section(e4.reshape(1, nblocks, BLK, width), table_q),
        "seq",
        split_axis=2,
        concat_axis=1,
        tiled=True,
    )
    grad_back = lax.all_to_all(
        span_section(grad_cols, filt, table_p), "seq", split_axis=1, concat_axis=2, tiled=True
    )
    dw = final_section(grad_back, table_q).reshape(tok, width)
    mixed = (g_part * h4).astype(jnp.bfloat16)
    ds = jnp.concatenate([dw * v_part, gradf * h4, dw * a_part], axis=1).astype(jnp.bfloat16)
    dspad = padded(ds, (("seq", 0),), 1)
    du = (taps[0] * dspad[2:] + taps[1] * dspad[1:-1] + taps[2] * dspad[:-2]).astype(jnp.bfloat16)
    in_grad = jnp.dot(du, w_in.T, preferred_element_type=jnp.float32).astype(jnp.bfloat16)
    dsf = ds.astype(jnp.float32)
    zf = zpad.astype(jnp.float32)
    local_taps = jnp.stack([jnp.sum(dsf * zf[k : k + tok], axis=0) for k in range(3)])
    taps_grad = lax.psum(local_taps, ("dp", "seq")) * factor
    contract = (((0,), (0,)), ((), ()))
    partial_sum = lax.psum_scatter(
        lax.dot_general(rows, du, contract, preferred_element_type=jnp.float32),
        "dp",
        scatter_dimension=0,
        tiled=True,
    )
    w_grad = lax.psum_scatter(partial_sum, "seq", scatter_dimension=1, tiled=True) * factor
    return (mixed[None], in_grad[None], w_grad, taps_grad)


def solution(mesh):
    return jax.shard_map(
        shards,
        mesh=mesh,
        in_specs=(P("dp", "seq", None), P("dp", "seq", None), P(), P(), P(None, "seq", None)),
        out_specs=(P("dp", "seq", None), P("dp", "seq", None), P("dp", "seq"), P()),
        check_vma=False,
    )
```

profile of v0, /device:TPU:2, one launch (start us, length us, event | category | flops | bytes accessed | tf_op | source)
XLA Modules:
  0.0 500.8 jit_solution(6452901341456452620)
XLA Ops:
  7.2 0.0 copy-start
  7.2 0.0 copy-start.12
  7.2 1.2 copy-done
  8.4 6.4 %convolution_convert_fusion.2 = bf16[512,3072]{1,0:T(8,128)(2,1)S(1)} fusion(bf16[1024,3072]{1,0:T(8,128)(2,1)} %param.7, bf16[1,512,1024]{2,1,0:T(8,128)(2,1)S(1)} %copy-done), kind=kOutput, calls=%fused_computation.22 | convolution fusion | flops 3222798336 | bytes 10485760 | tf_op jit(solution)/shard_map/dot_general | solution.py:72
  14.8 0.0 copy-start.9
  14.9 2.0 collective-permute-start
  16.9 1.3 collective-permute-start.1
  18.2 0.0 copy-done.12
  18.2 0.0 collective-permute-done
  18.2 3.4 collective-permute-done.1
  21.6 2.5 multiply_add_fusion
  24.2 2.7 copy-done.2
  26.8 0.0 copy-done.9
  26.8 0.3 fusion.12
  27.2 1.4 fusion.19
  28.6 2.1 copy.34
  30.7 11.8 %all-to-all-start.2 = ((bf16[1,2,256,1024]{3,1,0,2:T(2,128)(2,1)}), bf16[1,2,256,1024]{3,1,0,2:T(2,128)(2,1)S(1)}, u32[]{:S(2)}, u32[]{:S(2)}) async-start(bf16[1,2,256,1024]{3,1,0,2:T(2,128)(2,1)} %copy.34), calls=%async_computation.2 | async-start | bytes 2097152 | tf_op jit(solution)/shard_map/all_to_all | solution.py:92
  42.5 0.0 reduce-scatter.3.cloned.1.call-start
  42.5 0.0 copy-done.11
  42.6 1.6 reshape.130
  44.2 26.7 %all-to-all-done.2 = bf16[1,2,256,1024]{3,1,0,2:T(2,128)(2,1)S(1)} async-done(((bf16[1,2,256,1024]{3,1,0,2:T(2,128)(2,1)}), bf16[1,2,256,1024]{3,1,0,2:T(2,128)(2,1)S(1)}, u32[]{:S(2)}, u32[]{:S(2)}) %all-to-all-start.2) | async-done | bytes 1048608 | tf_op jit(solution)/shard_map/all_to_all | solution.py:92
  70.9 0.3 copy.59
  71.1 0.1 copy.36
  71.2 0.0 slice-start
  71.2 1.6 copy.47
  72.8 3.8 convolution_convert_fusion
  76.7 2.0 copy.48
  78.6 0.1 bitcast_bitcast_fusion
  78.7 32.2 %all_to_all.60 = bf16[1,64,8,1024]{3,2,0,1:T(8,128)(2,1)S(1)} all-to-all(bf16[1,64,8,1024]{3,2,0,1:T(8,128)(2,1)S(1)} %bitcast_bitcast_fusion), channel_id=1, replica_groups=mesh['dp'=8,'seq'=32] {'seq'}, dimensions={1} | all-to-all | bytes 2097152 | tf_op jit(solution)/shard_map/all_to_all | solution.py:99
  111.0 1.3 fusion.20
  112.3 2.2 fusion.14
  114.5 2.4 fusion.18
  116.9 3.7 copy.27
  120.6 32.4 %all_to_all.61 = bf16[1,2,256,1024]{3,1,0,2:T(2,128)(2,1)S(1)} all-to-all(bf16[1,2,256,1024]{3,1,0,2:T(2,128)(2,1)} %copy.27), channel_id=1, replica_groups=mesh['dp'=8,'seq'=32] {'seq'}, dimensions={2} | all-to-all | bytes 2097152 | tf_op jit(solution)/shard_map/all_to_all | solution.py:81
  153.1 0.3 copy.60
  153.4 0.1 copy.29
  153.4 1.6 copy.45
  155.0 0.0 copy-done.3
  155.0 3.2 convolution_convert_fusion.1
  158.2 1.9 copy.46
  160.1 0.1 bitcast_bitcast_fusion.1
  160.2 0.0 copy-start.5
  160.2 32.4 %all_to_all.62 = bf16[1,64,8,1024]{3,2,0,1:T(8,128)(2,1)S(1)} all-to-all(bf16[1,64,8,1024]{3,2,0,1:T(8,128)(2,1)S(1)} %bitcast_bitcast_fusion.1), channel_id=1, replica_groups=mesh['dp'=8,'seq'=32] {'seq'}, dimensions={1} | all-to-all | bytes 2097152 | tf_op jit(solution)/shard_map/all_to_all | solution.py:88
  192.6 1.3 fusion.22
  193.9 3.2 fusion.13
  197.1 0.0 copy-done.5
  197.2 0.3 pad_maximum_fusion.8
  197.4 1.3 collective-permute-start.2
  198.7 3.0 collective-permute-start.3
  201.8 0.0 collective-permute-done.2
  201.8 0.8 collective-permute-done.3
  202.6 0.0 copy-done.7
  202.6 12.4 %convolution_bitcast_fusion.2 = f32[1024,3072]{0,1:T(8,128)} fusion(bf16[1,512,1024]{2,1,0:T(8,128)(2,1)S(1)} %copy-done, bf16[1,3072]{1,0:T(2,128)(2,1)S(1)} %collective-permute-done.3, bf16[512,1024]{1,0:T(8,128)(2,1)S(1)} %copy-done.6, bf16[512,1024]{1,0:T(8,128)(2,1)S(1)} %get-tuple-element.14, bf16[512,1024]{1,0:T(8,128)(2,1)S(1)} %copy-done.5, ...), kind=kOutput, calls=%fused_computation.14 | convolution fusion | flops 3265265664 | bytes 16826368 | tf_op jit(solution)/shard_map/dot_general | solution.py:114
  215.0 0.0 reduce-scatter.3.cloned.1.call-update
  215.0 0.3 reduce-scatter.5.cloned.1.call-start
  215.3 5.5 %maximum_convert_fusion = f32[514,3072]{1,0:T(8,128)} fusion(bf16[1,3072]{1,0:T(2,128)(2,1)S(1)} %collective-permute-done.1, bf16[512,3072]{1,0:T(8,128)(2,1)} %copy-done.4, bf16[1,3072]{1,0:T(2,128)(2,1)S(1)} %collective-permute-done), kind=kLoop, calls=%fused_computation.23 | loop fusion | flops 9474048 | bytes 9474048 | tf_op jit(solution)/shard_map/convert_element_type | solution.py:109
  220.7 152.5 %reduce-scatter.3.cloned.1.call-done = f32[128,3072]{0,1:T(8,128)} async-done(((f32[1024,3072]{0,1:T(8,128)}), f32[128,3072]{0,1:T(8,128)}) %reduce-scatter.3.cloned.1.call-update) | async-done | bytes 1572880 | tf_op jit(solution)/shard_map/reduce_scatter | solution.py:113
  373.3 0.0 reduce-scatter.5.cloned.1.call-update
  373.3 9.3 %fusion.9 = (f32[3072]{0:T(1024)S(1)}, f32[3072]{0:T(1024)S(1)}, f32[3072]{0:T(1024)S(1)}) fusion(f32[514,3072]{1,0:T(8,128)} %maximum_convert_fusion, bf16[512,1024]{1,0:T(8,128)(2,1)S(1)} %copy-done.6, bf16[512,1024]{1,0:T(8,128)(2,1)S(1)} %copy-done.8, bf16[512,1024]{1,0:T(8,128)(2,1)S(1)} %copy-done.5), kind=kLoop, calls=%fused_computation.18 | loop fusion | flops 18865152 | bytes 22056960 | tf_op jit(solution)/shard_map/reduce_sum | solution.py:110
  382.7 75.7 %psum.7 = f32[3,3072]{1,0:T(4,128)S(1)} all-reduce(f32[3,3072]{1,0:T(4,128)S(1)} %pad_maximum_fusion.9), channel_id=1, replica_groups=mesh['dp'=8,'seq'=32] {'dp','seq'}, use_global_device_ids=true, to_apply=%region_5.6 | all-reduce | flops 9216 | bytes 73728 | tf_op jit(solution)/shard_map/psum | solution.py:111
  458.4 0.6 broadcast_multiply_fusion
  459.0 11.0 %fusion.17 = bf16[1,512,1024]{2,1,0:T(8,128)(2,1)} fusion(bf16[1024,3072]{1,0:T(8,128)(2,1)} %param.7, bf16[1,3072]{1,0:T(2,128)(2,1)S(1)} %collective-permute-done.3, bf16[512,1024]{1,0:T(8,128)(2,1)S(1)} %copy-done.6, bf16[512,1024]{1,0:T(8,128)(2,1)} %copy-done.7, bf16[512,1024]{1,0:T(8,128)(2,1)S(1)} %copy-done.5, ...), kind=kOutput, calls=%fused_computation.47 | convolution fusion | flops 3265789952 | bytes 10534912 | tf_op jit(solution)/shard_map/dot_general | solution.py:107
  470.0 22.5 %reduce-scatter.5.cloned.1.call-done = f32[128,96]{0,1:T(8,128)} async-done(((f32[128,3072]{0,1:T(8,128)}), f32[128,96]{0,1:T(8,128)}) %reduce-scatter.5.cloned.1.call-update) | async-done | bytes 49168 | tf_op jit(solution)/shard_map/reduce_scatter | solution.py:119
  492.5 1.4 broadcast_multiply_fusion.1
  (24 shorter events, 0.2 us)
Async XLA Ops:
  7.2 1.2 copy-start
  7.2 11.0 %copy-start.12 = (f32[3,3072]{1,0:T(4,128)S(1)}, f32[3,3072]{1,0:T(4,128)}, u32[]{:S(2)}) copy-start(f32[3,3072]{1,0:T(4,128)} %param.8) | copy-start | bytes 110596
  14.8 12.4 %copy-start.4 = (bf16[512,3072]{1,0:T(8,128)(2,1)}, bf16[512,3072]{1,0:T(8,128)(2,1)S(1)}, u32[]{:S(2)}) copy-start(bf16[512,3072]{1,0:T(8,128)(2,1)S(1)} %convolution_convert_fusion.2) | copy-start | bytes 9437188
  14.8 12.0 %copy-start.9 = (bf16[1,512,1024]{2,1,0:T(8,128)(2,1)S(1)}, bf16[1,512,1024]{2,1,0:T(8,128)(2,1)}, u32[]{:S(2)}) copy-start(bf16[1,512,1024]{2,1,0:T(8,128)(2,1)} %param.6) | copy-start | bytes 3145732
  14.9 3.4 collective-permute-start
  16.9 4.8 collective-permute-start.1
  24.2 2.7 copy-start.2
  26.8 15.7 %copy-start.11 = (bf16[64,8,1024]{2,1,0:T(8,128)(2,1)S(1)}, bf16[64,8,1024]{2,1,0:T(8,128)(2,1)}, u32[]{:S(2)}) copy-start(bf16[64,8,1024]{2,1,0:T(8,128)(2,1)} %param.9) | copy-start | bytes 3145732
  30.7 40.1 %all-to-all-start.2 = ((bf16[1,2,256,1024]{3,1,0,2:T(2,128)(2,1)}), bf16[1,2,256,1024]{3,1,0,2:T(2,128)(2,1)S(1)}, u32[]{:S(2)}, u32[]{:S(2)}) async-start(bf16[1,2,256,1024]{3,1,0,2:T(2,128)(2,1)} %copy.34), calls=%async_computation.2 | async-start | bytes 2097152 | tf_op jit(solution)/shard_map/all_to_all | solution.py:92
  42.5 330.8 %reduce-scatter.3.cloned.1.call-start = ((), (), s32[]{:S(2)}) async-start(), calls=%async_computation.6 | async-start | bytes 14155776 | tf_op jit(solution)/shard_map/reduce_scatter | solution.py:113
  71.2 41.1 %slice-start = ((s8[6291456]{0:T(1024)(128)(4,1)}), s8[2097152]{0:T(1024)(128)(4,1)S(1)}, s32[]{:S(2)}) async-start(s8[6291456]{0:T(1024)(128)(4,1)} %bitcast.146), calls=%async_computation.8 | async-start | bytes 4194304
  76.7 35.6 %slice-start.1 = ((s8[6291456]{0:T(1024)(128)(4,1)}), s8[4194304]{0:T(1024)(128)(4,1)S(1)}, s32[]{:S(2)}) async-start(s8[6291456]{0:T(1024)(128)(4,1)} %bitcast.146), calls=%async_computation.9 | async-start | bytes 8388608
  114.5 40.5 %copy-start.3 = (f32[1,64,8192]{2,1,0:T(8,128)S(1)}, f32[1,64,8192]{2,1,0:T(8,128)}, u32[]{:S(2)}) copy-start(f32[1,64,8192]{2,1,0:T(8,128)} %reshape.130) | copy-start | bytes 6291460
  158.2 35.7 %copy-start.10 = (bf16[1,512,1024]{2,1,0:T(8,128)(2,1)S(1)}, bf16[1,512,1024]{2,1,0:T(8,128)(2,1)}, u32[]{:S(2)}) copy-start(bf16[1,512,1024]{2,1,0:T(8,128)(2,1)} %param.6) | copy-start | bytes 3145732
  160.2 37.0 %copy-start.5 = (bf16[512,1024]{1,0:T(8,128)(2,1)S(1)}, bf16[512,1024]{1,0:T(8,128)(2,1)}, u32[]{:S(2)}) copy-start(bf16[512,1024]{1,0:T(8,128)(2,1)} %get-tuple-element.7) | copy-start | bytes 3145732
  160.2 37.0 %copy-start.6 = (bf16[512,1024]{1,0:T(8,128)(2,1)S(1)}, bf16[512,1024]{1,0:T(8,128)(2,1)}, u32[]{:S(2)}) copy-start(bf16[512,1024]{1,0:T(8,128)(2,1)} %get-tuple-element.8) | copy-start | bytes 3145732
  197.1 5.5 %copy-start.7 = (bf16[512,1024]{1,0:T(8,128)(2,1)}, bf16[512,1024]{1,0:T(8,128)(2,1)S(1)}, u32[]{:S(2)}) copy-start(bf16[512,1024]{1,0:T(8,128)(2,1)S(1)} %get-tuple-element.14) | copy-start | bytes 3145732
  197.4 4.3 collective-permute-start.2
  198.7 3.9 collective-permute-start.3
  215.0 158.3 %copy-start.8 = (bf16[512,1024]{1,0:T(8,128)(2,1)S(1)}, bf16[512,1024]{1,0:T(8,128)(2,1)}, u32[]{:S(2)}) copy-start(bf16[512,1024]{1,0:T(8,128)(2,1)} %copy-done.7) | copy-start | bytes 3145732
  215.0 277.5 %reduce-scatter.5.cloned.1.call-start = ((), (), s32[]{:S(2)}) async-start(), calls=%async_computation.7 | async-start | bytes 1622016 | tf_op jit(solution)/shard_map/reduce_scatter | solution.py:119
  459.0 35.0 %copy-start.1 = (bf16[1,512,1024]{2,1,0:T(8,128)(2,1)S(1)}, bf16[1,512,1024]{2,1,0:T(8,128)(2,1)}, u32[]{:S(2)}) copy-start(bf16[1,512,1024]{2,1,0:T(8,128)(2,1)} %param.5) | copy-start | bytes 3145732
Sparse Core Ops, SparseCore 0:
  215.1 158.0 reduce-scatter.2
  375.9 116.5 reduce-scatter.4
where the time goes:
time: 502 us; the launch traced here: 501 us
  waiting for transfers between devices  206 us (41%)
  blocking collectives  173 us (34%)
  matrix products  43.3 us (9%)
  other arithmetic  25.5 us (5%)
  starting transfers between devices  19.7 us (4%)
  local copies, waits for them, and re-layouts  19.3 us (4%)
  between operations  14.4 us (3%)
    reduce_scatter x1, waiting for transfers between devices, shards(): lax.psum_scatter(lax.dot_general(rows, du, contract, preferred_element_ty...  153 us
    psum x1, blocking collectives, shards(): taps_grad = lax.psum(local_taps, ('dp', 'seq')) * factor  75.7 us
    all_to_all x1, blocking collectives, shards(): lax.all_to_all(block_section(w.reshape(1, nblocks, BLK, width), table_q),...  32.4 us
    all_to_all x1, blocking collectives, shards(): lax.all_to_all(span_section(columns, filt, table_p), 'seq', split_axis=1,...  32.4 us
    all_to_all x1, blocking collectives, shards(): lax.all_to_all(span_section(grad_cols, filt, table_p), 'seq', split_axis=...  32.2 us
    all_to_all x1, waiting for transfers between devices, shards(): lax.all_to_all(block_section(e4.reshape(1, nblocks, BLK, width), table_q)...  26.7 us
    reduce_scatter x1, waiting for transfers between devices, shards(): lax.psum_scatter(partial_sum, 'seq', scatter_dimension=1, tiled=True)  22.5 us
    dot_general x1, matrix products, shards(): lax.dot_general(rows, du, contract, preferred_element_type=jnp.float32)  12.4 us
  transfers between devices with their start and end apart: 7, of which 5 were waited for; matrix products, arithmetic and copies ran while one was open for 6% of the time, Pallas kernels for 0%

commit v1 on v0

--- a/solution.py
+++ b/solution.py
@@ -1,3 +1,4 @@
+import functools
 import math
 import jax
 import jax.numpy as jnp
@@ -5,6 +6,14 @@
 from jax.sharding import PartitionSpec as P
 
 BLK = 256
+
+
+def _supply_all_core(x0, across, comm_axis):
+    after = lax.psum(x0, axis_name=across)
+    return lax.psum(after, axis_name=comm_axis)
+
+
+read_panels = functools.partial(_supply_all_core, across="dp", comm_axis="seq")
 
 
 def padded(cells, sides, width):
@@ -108,7 +117,7 @@
     dsf = ds.astype(jnp.float32)
     zf = zpad.astype(jnp.float32)
     local_taps = jnp.stack([jnp.sum(dsf * zf[k : k + tok], axis=0) for k in range(3)])
-    taps_grad = lax.psum(local_taps, ("dp", "seq")) * factor
+    taps_grad = read_panels(local_taps) * factor
     contract = (((0,), (0,)), ((), ()))
     partial_sum = lax.psum_scatter(
         lax.dot_general(rows, du, contract, preferred_element_type=jnp.float32),

time: 502 us -> 547 us (1.090)
  blocking collectives: 173 us -> 239 us
  waiting for transfers between devices: 206 us -> 184 us
    psum x1 -> x2, blocking collectives: 75.7 us -> 142 us  [the longest x1 105 us: _supply_all_core(): return lax.psum(after, axis_name=comm_axis)]
    reduce_scatter x1, waiting for transfers between devices: 22.5 us -> 0.01 us  [shards(): lax.psum_scatter(partial_sum, 'seq', scatter_dimension=1, tiled=True)]
  transfers between devices with their start and end apart: 7 -> 7, of which waited for: 5 -> 4; matrix products, arithmetic and copies ran while one was open for 6% -> 5% of each run, Pallas kernels for 0% -> 0%
where the time goes in v1:
time: 547 us; the launch traced here: 545 us
  blocking collectives  239 us (44%)
  waiting for transfers between devices  184 us (34%)
  matrix products  43.2 us (8%)
  other arithmetic  25.5 us (5%)
  starting transfers between devices  19.7 us (4%)
  local copies, waits for them, and re-layouts  19.3 us (4%)
  between operations  14.4 us (3%)
    reduce_scatter x1, waiting for transfers between devices, shards(): lax.psum_scatter(lax.dot_general(rows, du, contract, preferred_element_ty...  153 us
    psum x1, blocking collectives, _supply_all_core(): return lax.psum(after, axis_name=comm_axis)  105 us
    psum x1, blocking collectives, _supply_all_core(): after = lax.psum(x0, axis_name=across)  36.9 us
    all_to_all x1, blocking collectives, shards(): lax.all_to_all(block_section(w.reshape(1, nblocks, BLK, width), table_q),...  32.5 us
    all_to_all x1, blocking collectives, shards(): lax.all_to_all(span_section(columns, filt, table_p), 'seq', split_axis=1,...  32.4 us
    all_to_all x1, blocking collectives, shards(): lax.all_to_all(span_section(grad_cols, filt, table_p), 'seq', split_axis=...  32.2 us
    all_to_all x1, waiting for transfers between devices, shards(): lax.all_to_all(block_section(e4.reshape(1, nblocks, BLK, width), table_q)...  26.7 us
    dot_general x1, matrix products, shards(): lax.dot_general(rows, du, contract, preferred_element_type=jnp.float32)  12.3 us
  transfers between devices with their start and end apart: 7, of which 4 were waited for; matrix products, arithmetic and copies ran while one was open for 5% of the time, Pallas kernels for 0%

profile of v1, /device:TPU:2, one launch (start us, length us, event | category | flops | bytes accessed | tf_op | source)
XLA Modules:
  0.0 544.7 jit_solution(9649329210118510357)
XLA Ops:
  7.2 0.0 copy-start
  7.2 0.0 copy-start.12
  7.2 1.2 copy-done
  8.4 6.4 %convolution_convert_fusion.2 = bf16[512,3072]{1,0:T(8,128)(2,1)S(1)} fusion(bf16[1024,3072]{1,0:T(8,128)(2,1)} %param.7, bf16[1,512,1024]{2,1,0:T(8,128)(2,1)S(1)} %copy-done), kind=kOutput, calls=%fused_computation.22 | convolution fusion | flops 3222798336 | bytes 10485760 | tf_op jit(solution)/shard_map/dot_general | solution.py:81
  14.8 0.0 copy-start.4
  14.8 0.0 copy-start.9
  14.9 2.0 collective-permute-start
  16.9 1.3 collective-permute-start.1
  18.2 0.0 copy-done.12
  18.2 0.0 collective-permute-done
  18.2 3.4 collective-permute-done.1
  21.6 2.5 multiply_add_fusion
  24.2 0.0 copy-start.2
  24.2 2.7 copy-done.2
  26.8 0.3 fusion.12
  27.2 1.4 fusion.19
  28.6 2.1 copy.34
  30.7 11.8 %all-to-all-start.2 = ((bf16[1,2,256,1024]{3,1,0,2:T(2,128)(2,1)}), bf16[1,2,256,1024]{3,1,0,2:T(2,128)(2,1)S(1)}, u32[]{:S(2)}, u32[]{:S(2)}) async-start(bf16[1,2,256,1024]{3,1,0,2:T(2,128)(2,1)} %copy.34), calls=%async_computation.2 | async-start | bytes 2097152 | tf_op jit(solution)/shard_map/all_to_all | solution.py:101
  42.5 0.0 reduce-scatter.3.cloned.1.call-start
  42.5 0.0 copy-done.11
  42.6 1.6 reshape.130
  44.1 26.7 %all-to-all-done.2 = bf16[1,2,256,1024]{3,1,0,2:T(2,128)(2,1)S(1)} async-done(((bf16[1,2,256,1024]{3,1,0,2:T(2,128)(2,1)}), bf16[1,2,256,1024]{3,1,0,2:T(2,128)(2,1)S(1)}, u32[]{:S(2)}, u32[]{:S(2)}) %all-to-all-start.2) | async-done | bytes 1048608 | tf_op jit(solution)/shard_map/all_to_all | solution.py:101
  70.9 0.3 copy.59
  71.1 0.1 copy.36
  71.2 0.0 slice-start
  71.2 1.6 copy.47
  72.8 3.8 convolution_convert_fusion
  76.7 2.0 copy.48
  78.6 0.1 bitcast_bitcast_fusion
  78.7 32.2 %all_to_all.60 = bf16[1,64,8,1024]{3,2,0,1:T(8,128)(2,1)S(1)} all-to-all(bf16[1,64,8,1024]{3,2,0,1:T(8,128)(2,1)S(1)} %bitcast_bitcast_fusion), channel_id=1, replica_groups=mesh['dp'=8,'seq'=32] {'seq'}, dimensions={1} | all-to-all | bytes 2097152 | tf_op jit(solution)/shard_map/all_to_all | solution.py:108
  111.0 1.3 fusion.20
  112.3 2.2 fusion.14
  114.6 2.4 fusion.18
  116.9 3.7 copy.27
  120.7 32.5 %all_to_all.61 = bf16[1,2,256,1024]{3,1,0,2:T(2,128)(2,1)S(1)} all-to-all(bf16[1,2,256,1024]{3,1,0,2:T(2,128)(2,1)} %copy.27), channel_id=1, replica_groups=mesh['dp'=8,'seq'=32] {'seq'}, dimensions={2} | all-to-all | bytes 2097152 | tf_op jit(solution)/shard_map/all_to_all | solution.py:90
  153.1 0.3 copy.60
  153.4 0.1 copy.29
  153.5 1.6 copy.45
  155.1 0.0 copy-done.3
  155.1 3.2 convolution_convert_fusion.1
  158.2 1.9 copy.46
  160.2 0.1 bitcast_bitcast_fusion.1
  160.2 0.0 copy-start.5
  160.3 32.4 %all_to_all.62 = bf16[1,64,8,1024]{3,2,0,1:T(8,128)(2,1)S(1)} all-to-all(bf16[1,64,8,1024]{3,2,0,1:T(8,128)(2,1)S(1)} %bitcast_bitcast_fusion.1), channel_id=1, replica_groups=mesh['dp'=8,'seq'=32] {'seq'}, dimensions={1} | all-to-all | bytes 2097152 | tf_op jit(solution)/shard_map/all_to_all | solution.py:97
  192.6 1.3 fusion.22
  194.0 3.2 fusion.13
  197.2 0.0 copy-done.6
  197.2 0.3 pad_maximum_fusion.8
  197.5 1.3 collective-permute-start.2
  198.8 3.0 collective-permute-start.3
  201.8 0.0 collective-permute-done.2
  201.9 0.8 collective-permute-done.3
  202.7 12.3 %convolution_bitcast_fusion.2 = f32[1024,3072]{0,1:T(8,128)} fusion(bf16[1,512,1024]{2,1,0:T(8,128)(2,1)S(1)} %copy-done, bf16[1,3072]{1,0:T(2,128)(2,1)S(1)} %collective-permute-done.3, bf16[512,1024]{1,0:T(8,128)(2,1)S(1)} %copy-done.6, bf16[512,1024]{1,0:T(8,128)(2,1)S(1)} %get-tuple-element.14, bf16[512,1024]{1,0:T(8,128)(2,1)S(1)} %copy-done.5, ...), kind=kOutput, calls=%fused_computation.14 | convolution fusion | flops 3265265664 | bytes 16826368 | tf_op jit(solution)/shard_map/dot_general | solution.py:123
  215.0 0.0 reduce-scatter.3.cloned.1.call-update
  215.0 0.3 reduce-scatter.5.cloned.1.call-start
  215.3 5.5 %maximum_convert_fusion = f32[514,3072]{1,0:T(8,128)} fusion(bf16[1,3072]{1,0:T(2,128)(2,1)S(1)} %collective-permute-done.1, bf16[512,3072]{1,0:T(8,128)(2,1)} %copy-done.4, bf16[1,3072]{1,0:T(2,128)(2,1)S(1)} %collective-permute-done), kind=kLoop, calls=%fused_computation.23 | loop fusion | flops 9474048 | bytes 9474048 | tf_op jit(solution)/shard_map/convert_element_type | solution.py:118
  220.8 152.6 %reduce-scatter.3.cloned.1.call-done = f32[128,3072]{0,1:T(8,128)} async-done(((f32[1024,3072]{0,1:T(8,128)}), f32[128,3072]{0,1:T(8,128)}) %reduce-scatter.3.cloned.1.call-update) | async-done | bytes 1572880 | tf_op jit(solution)/shard_map/reduce_scatter | solution.py:122
  373.4 0.0 reduce-scatter.5.cloned.1.call-update
  373.4 9.3 %fusion.9 = (f32[3072]{0:T(1024)S(1)}, f32[3072]{0:T(1024)S(1)}, f32[3072]{0:T(1024)S(1)}) fusion(f32[514,3072]{1,0:T(8,128)} %maximum_convert_fusion, bf16[512,1024]{1,0:T(8,128)(2,1)S(1)} %copy-done.6, bf16[512,1024]{1,0:T(8,128)(2,1)S(1)} %copy-done.8, bf16[512,1024]{1,0:T(8,128)(2,1)S(1)} %copy-done.5), kind=kLoop, calls=%fused_computation.18 | loop fusion | flops 18865152 | bytes 22056960 | tf_op jit(solution)/shard_map/reduce_sum | solution.py:119
  382.8 36.9 %psum.14 = f32[3,3072]{1,0:T(4,128)S(1)} all-reduce(f32[3,3072]{1,0:T(4,128)S(1)} %pad_maximum_fusion.9), channel_id=1, replica_groups=mesh['dp'=8,'seq'=32] {'dp'}, use_global_device_ids=true, to_apply=%region_5.6 | all-reduce | flops 9216 | bytes 73728 | tf_op jit(solution)/shard_map/psum | solution.py:12
  419.7 105.1 %psum.15 = f32[3,3072]{1,0:T(4,128)S(1)} all-reduce(f32[3,3072]{1,0:T(4,128)S(1)} %psum.14), channel_id=1, replica_groups=mesh['dp'=8,'seq'=32] {'seq'}, use_global_device_ids=true, to_apply=%region_6.7 | all-reduce | flops 9216 | bytes 73728 | tf_op jit(solution)/shard_map/psum | solution.py:13
  524.8 0.6 broadcast_multiply_fusion
  525.4 11.0 %fusion.17 = bf16[1,512,1024]{2,1,0:T(8,128)(2,1)} fusion(bf16[1024,3072]{1,0:T(8,128)(2,1)} %param.7, bf16[1,3072]{1,0:T(2,128)(2,1)S(1)} %collective-permute-done.3, bf16[512,1024]{1,0:T(8,128)(2,1)S(1)} %copy-done.6, bf16[512,1024]{1,0:T(8,128)(2,1)} %copy-done.7, bf16[512,1024]{1,0:T(8,128)(2,1)S(1)} %copy-done.5, ...), kind=kOutput, calls=%fused_computation.47 | convolution fusion | flops 3265789952 | bytes 10534912 | tf_op jit(solution)/shard_map/dot_general | solution.py:116
  536.4 1.4 broadcast_multiply_fusion.1
  (25 shorter events, 0.2 us)
Async XLA Ops:
  7.2 1.2 copy-start
  7.2 11.0 %copy-start.12 = (f32[3,3072]{1,0:T(4,128)S(1)}, f32[3,3072]{1,0:T(4,128)}, u32[]{:S(2)}) copy-start(f32[3,3072]{1,0:T(4,128)} %param.8) | copy-start | bytes 110596
  14.8 12.4 %copy-start.4 = (bf16[512,3072]{1,0:T(8,128)(2,1)}, bf16[512,3072]{1,0:T(8,128)(2,1)S(1)}, u32[]{:S(2)}) copy-start(bf16[512,3072]{1,0:T(8,128)(2,1)S(1)} %convolution_convert_fusion.2) | copy-start | bytes 9437188
  14.8 12.0 %copy-start.9 = (bf16[1,512,1024]{2,1,0:T(8,128)(2,1)S(1)}, bf16[1,512,1024]{2,1,0:T(8,128)(2,1)}, u32[]{:S(2)}) copy-start(bf16[1,512,1024]{2,1,0:T(8,128)(2,1)} %param.6) | copy-start | bytes 3145732
  14.9 3.4 collective-permute-start
  16.9 4.8 collective-permute-start.1
  24.2 2.7 copy-start.2
  26.8 15.7 %copy-start.11 = (bf16[64,8,1024]{2,1,0:T(8,128)(2,1)S(1)}, bf16[64,8,1024]{2,1,0:T(8,128)(2,1)}, u32[]{:S(2)}) copy-start(bf16[64,8,1024]{2,1,0:T(8,128)(2,1)} %param.9) | copy-start | bytes 3145732
  30.7 40.2 %all-to-all-start.2 = ((bf16[1,2,256,1024]{3,1,0,2:T(2,128)(2,1)}), bf16[1,2,256,1024]{3,1,0,2:T(2,128)(2,1)S(1)}, u32[]{:S(2)}, u32[]{:S(2)}) async-start(bf16[1,2,256,1024]{3,1,0,2:T(2,128)(2,1)} %copy.34), calls=%async_computation.2 | async-start | bytes 2097152 | tf_op jit(solution)/shard_map/all_to_all | solution.py:101
  42.5 330.9 %reduce-scatter.3.cloned.1.call-start = ((), (), s32[]{:S(2)}) async-start(), calls=%async_computation.6 | async-start | bytes 14155776 | tf_op jit(solution)/shard_map/reduce_scatter | solution.py:122
  71.2 41.1 %slice-start = ((s8[6291456]{0:T(1024)(128)(4,1)}), s8[2097152]{0:T(1024)(128)(4,1)S(1)}, s32[]{:S(2)}) async-start(s8[6291456]{0:T(1024)(128)(4,1)} %bitcast.146), calls=%async_computation.8 | async-start | bytes 4194304
  76.7 35.7 %slice-start.1 = ((s8[6291456]{0:T(1024)(128)(4,1)}), s8[4194304]{0:T(1024)(128)(4,1)S(1)}, s32[]{:S(2)}) async-start(s8[6291456]{0:T(1024)(128)(4,1)} %bitcast.146), calls=%async_computation.9 | async-start | bytes 8388608
  114.6 40.5 %copy-start.3 = (f32[1,64,8192]{2,1,0:T(8,128)S(1)}, f32[1,64,8192]{2,1,0:T(8,128)}, u32[]{:S(2)}) copy-start(f32[1,64,8192]{2,1,0:T(8,128)} %reshape.130) | copy-start | bytes 6291460
  158.2 35.7 %copy-start.10 = (bf16[1,512,1024]{2,1,0:T(8,128)(2,1)S(1)}, bf16[1,512,1024]{2,1,0:T(8,128)(2,1)}, u32[]{:S(2)}) copy-start(bf16[1,512,1024]{2,1,0:T(8,128)(2,1)} %param.6) | copy-start | bytes 3145732
  160.2 37.0 %copy-start.5 = (bf16[512,1024]{1,0:T(8,128)(2,1)S(1)}, bf16[512,1024]{1,0:T(8,128)(2,1)}, u32[]{:S(2)}) copy-start(bf16[512,1024]{1,0:T(8,128)(2,1)} %get-tuple-element.7) | copy-start | bytes 3145732
  160.2 37.0 %copy-start.6 = (bf16[512,1024]{1,0:T(8,128)(2,1)S(1)}, bf16[512,1024]{1,0:T(8,128)(2,1)}, u32[]{:S(2)}) copy-start(bf16[512,1024]{1,0:T(8,128)(2,1)} %get-tuple-element.8) | copy-start | bytes 3145732
  197.2 5.5 %copy-start.7 = (bf16[512,1024]{1,0:T(8,128)(2,1)}, bf16[512,1024]{1,0:T(8,128)(2,1)S(1)}, u32[]{:S(2)}) copy-start(bf16[512,1024]{1,0:T(8,128)(2,1)S(1)} %get-tuple-element.14) | copy-start | bytes 3145732
  197.5 4.3 collective-permute-start.2
  198.8 3.9 collective-permute-start.3
  215.0 158.3 %copy-start.8 = (bf16[512,1024]{1,0:T(8,128)(2,1)S(1)}, bf16[512,1024]{1,0:T(8,128)(2,1)}, u32[]{:S(2)}) copy-start(bf16[512,1024]{1,0:T(8,128)(2,1)} %copy-done.7) | copy-start | bytes 3145732
  215.0 321.4 %reduce-scatter.5.cloned.1.call-start = ((), (), s32[]{:S(2)}) async-start(), calls=%async_computation.7 | async-start | bytes 1622016 | tf_op jit(solution)/shard_map/reduce_scatter | solution.py:128
  525.4 12.4 %copy-start.1 = (bf16[1,512,1024]{2,1,0:T(8,128)(2,1)S(1)}, bf16[1,512,1024]{2,1,0:T(8,128)(2,1)}, u32[]{:S(2)}) copy-start(bf16[1,512,1024]{2,1,0:T(8,128)(2,1)} %param.5) | copy-start | bytes 3145732
Sparse Core Ops, SparseCore 0:
  215.2 158.1 reduce-scatter.2
  376.0 117.0 reduce-scatter.4
